TPU v7x, 32 devices: a whole 2x2x4 slice. The times are simulated.
32 devices in a mesh: slab: 8 (over y, x, core), lat: 4 (over z).
Axes of the slice: x: 2, y: 2, z: 4, core: 2. Of those that a mesh axis runs over, the one named last changes fastest.
Arguments:
- tokens: bfloat16 [16, 16, 16, 1024], P(None, 'lat', 'slab'), may hold values from -6 to 6
- conv_first: float32 [27, 1024], replicated, may hold values from -1.25 to 1.25
- conv_second: float32 [27, 1024], replicated, may hold values from -1.25 to 1.25
- kv_weight: bfloat16 [2, 1024, 1024], P(None, None, 'lat'), may hold values from -0.1875 to 0.1875
- queries: bfloat16 [512, 1024], replicated, may hold values from -70 to 70
Outputs:
- decoded: bfloat16 [16, 16, 16, 1024], P(None, 'lat', 'slab')
All inputs are finite; a program needn't handle non-finite values.
Results may differ from a plain program's by a relative error of at most 0.012.
The roundings to bfloat16 on the way count: a program that leaves them out, or rounds other values in their place, can miss the bound.
Values may be sent and summed in bfloat16 or wider, within the bound.
No kernel may reach another device: no remote copies, remote signals or barrier semaphores. Data moves between devices by JAX's collectives and lax.ppermute only.
A program may use at most 64 MiB of HBM per device.

v0:
```python
import jax
import jax.numpy as jnp
from jax import lax
from jax.sharding import PartitionSpec as P


def with_halo(block, sides, width):
    for axis, dim in sides:
        count = lax.axis_size(axis)
        forward = [(i, i + 1) for i in range(count - 1)]
        backward = [(target, source) for source, target in forward]
        low = lax.ppermute(
            lax.slice_in_dim(block, block.shape[dim] - width, None, axis=dim), axis, forward
        )
        high = lax.ppermute(lax.slice_in_dim(block, 0, width, axis=dim), axis, backward)
        block = jnp.concatenate([low, block, high], axis=dim)
    return block


def conv_valid(padded, weights):
    size_x = padded.shape[0] - 2
    size_y = padded.shape[1] - 2
    size_z = padded.shape[2] - 2
    accum_sum = jnp.zeros((size_x, size_y, size_z, padded.shape[3]), jnp.float32)
    for tap_index in range(27):
        shift_x = tap_index // 9
        shift_y = tap_index // 3 % 3
        shift_z = tap_index % 3
        window = padded[
            shift_x : shift_x + size_x, shift_y : shift_y + size_y, shift_z : shift_z + size_z
        ]
        accum_sum = accum_sum + weights[tap_index] * window
    return accum_sum


def extend_first(field):
    return jnp.pad(field.astype(jnp.float32), ((1, 1), (0, 0), (0, 0), (0, 0)))


def local(tokens, conv_first, conv_second, kv_weight, queries):
    width = tokens.shape[3]
    source = tokens.astype(jnp.float32)
    padded_tokens = with_halo(tokens, (("slab", 2), ("lat", 1)), 1)
    inner_layer = jax.nn.gelu(conv_valid(extend_first(padded_tokens), conv_first)).astype(
        jnp.bfloat16
    )
    beside_all = with_halo(inner_layer, (("slab", 2), ("lat", 1)), 1)
    mixed = jax.nn.gelu(conv_valid(extend_first(beside_all), conv_second))
    hidden = (source + mixed).astype(jnp.bfloat16)
    token_rows = hidden.reshape(-1, width)
    product = jnp.einsum(
        "td,kdw->ktw",
        token_rows,
        lax.all_gather(kv_weight, "lat", axis=2, tiled=True),
        preferred_element_type=jnp.float32,
    )
    projected = product.astype(jnp.bfloat16)
    key_rows = projected[0]
    value_rows = projected[1]
    score_scale = 1.0 / width**0.5
    scores = (
        jnp.einsum("ld,td->lt", queries, key_rows, preferred_element_type=jnp.float32) * score_scale
    )
    local_max = jnp.max(scores, axis=1)
    maximum = lax.pmax(local_max, ("slab", "lat"))
    exponent = jnp.exp(scores - maximum[:, None])
    weights_bf = exponent.astype(jnp.bfloat16)
    denominator = jnp.sum(exponent, axis=1)
    numerator = jnp.dot(weights_bf, value_rows, preferred_element_type=jnp.float32)
    numer_total, denom_total = lax.psum((numerator, denominator), ("slab", "lat"))
    latents = (numer_total / denom_total[:, None]).astype(jnp.bfloat16)
    back = (
        jnp.einsum("td,ld->tl", token_rows, latents, preferred_element_type=jnp.float32)
        * score_scale
    )
    probs = jax.nn.softmax(back, axis=1).astype(jnp.bfloat16)
    result = token_rows.astype(jnp.float32) + jnp.dot(
        probs, latents, preferred_element_type=jnp.float32
    )
    return result.astype(jnp.bfloat16).reshape(hidden.shape)


def solution(mesh):
    placed = (P(None, "lat", "slab", None), P(), P(), P(None, None, "lat"), P())
    return jax.shard_map(
        local, mesh=mesh, in_specs=placed, out_specs=P(None, "lat", "slab", None), check_vma=False
    )
```

profile of v0, /device:TPU:0, one launch (start us, length us, event | category | flops | bytes accessed | tf_op | source)
XLA Modules:
  0.0 288.1 jit_solution(4803963372032662820)
XLA Ops:
  7.3 1.6 fusion.90
  8.9 2.4 collective-permute-start
  11.4 1.3 collective-permute-start.1
  12.7 4.1 %collective-permute-done.1 = bf16[16,4,1,1024]{3,2,1,0:T(2,128)(2,1)S(1)} collective-permute-done((bf16[16,4,1,1024]{3,2,1,0:T(2,128)(2,1)S(1)}, bf16[16,4,1,1024]{3,2,1,0:T(2,128)(2,1)S(1)}, u32[]{:S(2)}, u32[]{:S(2)}) %collective-permute-start.1) | collective-permute-done | bytes 131104 | tf_op jit(solution)/shard_map/ppermute | solution.py:15
  17.3 3.5 %collective-permute-start.2 = (bf16[16,1,4,1024]{3,2,1,0:T(4,128)(2,1)S(1)}, bf16[16,1,4,1024]{3,2,1,0:T(4,128)(2,1)S(1)}, u32[]{:S(2)}, u32[]{:S(2)}) collective-permute-start(bf16[16,1,4,1024]{3,2,1,0:T(4,128)(2,1)S(1)} %get-tuple-element.7), channel_id=1, source_target_pairs={{0,1},{1,2},{2,3},{4,5},{5,6},{6,7},{8,9},{9,10},{10,11},{12,13},{... | collective-permute-start | bytes 393224 | tf_op jit(solution)/shard_map/ppermute | solution.py:12
  20.8 1.3 collective-permute-start.3
  22.2 4.1 %collective-permute-done.2 = bf16[16,1,4,1024]{3,2,1,0:T(4,128)(2,1)S(1)} collective-permute-done((bf16[16,1,4,1024]{3,2,1,0:T(4,128)(2,1)S(1)}, bf16[16,1,4,1024]{3,2,1,0:T(4,128)(2,1)S(1)}, u32[]{:S(2)}, u32[]{:S(2)}) %collective-permute-start.2) | collective-permute-done | bytes 131104 | tf_op jit(solution)/shard_map/ppermute | solution.py:12
  26.2 5.3 %collective-permute-done.3 = bf16[16,1,4,1024]{3,2,1,0:T(4,128)(2,1)S(1)} collective-permute-done((bf16[16,1,4,1024]{3,2,1,0:T(4,128)(2,1)S(1)}, bf16[16,1,4,1024]{3,2,1,0:T(4,128)(2,1)S(1)}, u32[]{:S(2)}, u32[]{:S(2)}) %collective-permute-start.3) | collective-permute-done | bytes 131104 | tf_op jit(solution)/shard_map/ppermute | solution.py:15
  32.5 6.8 %fusion.79 = bf16[16,4,2,1024]{3,2,1,0:T(2,128)(2,1)S(1)} fusion(f32[16,6,4,1024]{3,2,1,0:T(4,128)S(1)} %maximum_convert_fusion, f32[1024]{0:T(1024)S(1)} %bitcast.122, f32[1024]{0:T(1024)S(1)} %bitcast.123, f32[1024]{0:T(1024)S(1)} %bitcast.98, f32[1024]{0:T(1024)S(1)} %bitcast.99, f32[1024]{0:T(1024)S(1)} %bitcast.100, f32[1024]{0:T(1024)S(1)} %bitcast.101, ...), kind=kLoop, calls=%fused_computation.126 | loop fusion | flops 8126464 | bytes 6664192 | tf_op jit(solution)/shard_map/convert_element_type | solution.py:44
  39.9 6.2 %collective-permute-start.4 = (bf16[16,4,1,1024]{3,2,1,0:T(2,128)(2,1)S(1)}, bf16[16,4,1,1024]{3,2,1,0:T(2,128)(2,1)S(1)}, u32[]{:S(2)}, u32[]{:S(2)}) collective-permute-start(bf16[16,4,1,1024]{3,2,1,0:T(2,128)(2,1)S(1)} %get-tuple-element.9), channel_id=1, source_target_pairs={{0,4},{4,8},{8,12},{12,16},{16,20},{20,24},{24,28},{1,5},{5,9},{9,... | collective-permute-start | bytes 393224 | tf_op jit(solution)/shard_map/ppermute | solution.py:12
  46.1 1.3 collective-permute-start.5
  47.5 2.7 collective-permute-done.5
  50.7 8.4 %collective-permute-start.6 = (bf16[16,1,4,1024]{3,2,1,0:T(4,128)(2,1)S(1)}, bf16[16,1,4,1024]{3,2,1,0:T(4,128)(2,1)S(1)}, u32[]{:S(2)}, u32[]{:S(2)}) collective-permute-start(bf16[16,1,4,1024]{3,2,1,0:T(4,128)(2,1)S(1)} %get-tuple-element.5), channel_id=1, source_target_pairs={{0,1},{1,2},{2,3},{4,5},{5,6},{6,7},{8,9},{9,10},{10,11},{12,13},{... | collective-permute-start | bytes 393224 | tf_op jit(solution)/shard_map/ppermute | solution.py:12
  59.1 1.3 collective-permute-start.7
  60.4 4.1 %collective-permute-done.6 = bf16[16,1,4,1024]{3,2,1,0:T(4,128)(2,1)S(1)} collective-permute-done((bf16[16,1,4,1024]{3,2,1,0:T(4,128)(2,1)S(1)}, bf16[16,1,4,1024]{3,2,1,0:T(4,128)(2,1)S(1)}, u32[]{:S(2)}, u32[]{:S(2)}) %collective-permute-start.6) | collective-permute-done | bytes 131104 | tf_op jit(solution)/shard_map/ppermute | solution.py:12
  64.5 12.2 %collective-permute-done.7 = bf16[16,1,4,1024]{3,2,1,0:T(4,128)(2,1)S(1)} collective-permute-done((bf16[16,1,4,1024]{3,2,1,0:T(4,128)(2,1)S(1)}, bf16[16,1,4,1024]{3,2,1,0:T(4,128)(2,1)S(1)}, u32[]{:S(2)}, u32[]{:S(2)}) %collective-permute-start.7) | collective-permute-done | bytes 131104 | tf_op jit(solution)/shard_map/ppermute | solution.py:15
  77.7 7.0 %fusion.80 = bf16[16,4,2,1024]{3,2,1,0:T(2,128)(2,1)S(1)} fusion(f32[16,6,4,1024]{3,2,1,0:T(4,128)S(1)} %maximum_convert_fusion.1, bf16[16,4,2,1024]{3,2,1,0:T(2,128)(2,1)S(1)} %copy-done.1, f32[1024]{0:T(1024)S(1)} %bitcast.95, f32[1024]{0:T(1024)S(1)} %bitcast.96, f32[1024]{0:T(1024)S(1)} %bitcast.71, f32[1024]{0:T(1024)S(1)} %bitcast.72, ...), kind=kLoop, calls=%fused_computation.127 | loop fusion | flops 8388608 | bytes 6926336 | tf_op jit(solution)/shard_map/convert_element_type | solution.py:49
  84.8 13.0 %all-gather.2.cloned.1.call-done = bf16[2,1024,1024]{2,1,0:T(8,128)(2,1)} async-done(((bf16[2,1024,256]{2,1,0:T(8,128)(2,1)}), bf16[2,1024,1024]{2,1,0:T(8,128)(2,1)}) %all-gather.2.cloned.1.call-update) | async-done | bytes 4194320 | tf_op jit(solution)/shard_map/all_gather | solution.py:54
  97.8 2.9 %fusion = bf16[2,128,1024]{2,1,0:T(8,128)(2,1)S(1)} fusion(bf16[128,1024,1]{1,0,2:T(8,128)(2,1)S(1)} %reshape.66, bf16[2,1024,1024]{2,1,0:T(8,128)(2,1)} %all-gather.2.cloned.1.call-done), kind=kOutput, calls=%fused_computation.3 | convolution fusion | flops 537133056 | bytes 4980736 | tf_op jit(solution)/shard_map/td,kdw->ktw/dot_general | solution.py:51
  101.2 39.5 %pmax.7 = f32[512]{0:T(512)S(1)} all-reduce(f32[512]{0:T(512)S(1)} %get-tuple-element.67), channel_id=1, replica_groups=mesh['slab'=8,'lat'=4] {'slab','lat'}, use_global_device_ids=true, to_apply=%region_1.2 | all-reduce | flops 512 | bytes 4096 | tf_op jit(solution)/shard_map/pmax | solution.py:65
  140.7 1.8 fusion.81
  142.6 40.4 %psum.15 = f32[512]{0:T(512)S(1)} all-reduce(f32[512]{0:T(512)S(1)} %fusion.82), channel_id=1, replica_groups=mesh['slab'=8,'lat'=4] {'slab','lat'}, use_global_device_ids=true, to_apply=%region_4.5 | all-reduce | flops 512 | bytes 4096 | tf_op jit(solution)/shard_map/psum | solution.py:70
  183.1 94.3 %all-reduce.4.cloned.1.call-done = f32[512,1024]{1,0:T(8,128)} async-done(((f32[512,1024]{1,0:T(8,128)}), f32[512,1024]{1,0:T(8,128)}) %all-reduce.4.cloned.1.call-update) | async-done | bytes 2097168 | tf_op jit(solution)/shard_map/psum | solution.py:70
  277.4 1.9 divide_convert_fusion
  (31 shorter events, 7.0 us)
Async XLA Ops:
  6.5 94.1 %copy-start = (bf16[512,1024]{1,0:T(8,128)(2,1)S(1)}, bf16[512,1024]{1,0:T(8,128)(2,1)}, u32[]{:S(2)}) copy-start(bf16[512,1024]{1,0:T(8,128)(2,1)} %param.9) | copy-start | bytes 3145732
  6.5 10.3 %copy-start.1 = (bf16[16,4,2,1024]{3,2,1,0:T(2,128)(2,1)S(1)}, bf16[16,4,2,1024]{3,2,1,0:T(2,128)(2,1)}, u32[]{:S(2)}) copy-start(bf16[16,4,2,1024]{3,2,1,0:T(2,128)(2,1)} %param.5) | copy-start | bytes 786436
  6.5 6.1 %copy-start.2 = (f32[27,1024]{1,0:T(8,128)S(1)}, f32[27,1024]{1,0:T(8,128)}, u32[]{:S(2)}) copy-start(f32[27,1024]{1,0:T(8,128)} %param.6) | copy-start | bytes 331780
  6.5 91.2 %all-gather.2.cloned.1.call-start = ((), (), s32[]{:S(2)}) async-start(), calls=%async_computation | async-start | bytes 5242880 | tf_op jit(solution)/shard_map/all_gather | solution.py:54
  7.3 270.1 %all-reduce.4.cloned.1.call-start = ((), (), s32[]{:S(2)}) async-start(), calls=%async_computation.1 | async-start | bytes 4194304 | tf_op jit(solution)/shard_map/psum | solution.py:70
  8.9 3.8 %collective-permute-start = (bf16[16,4,1,1024]{3,2,1,0:T(2,128)(2,1)S(1)}, bf16[16,4,1,1024]{3,2,1,0:T(2,128)(2,1)S(1)}, u32[]{:S(2)}, u32[]{:S(2)}) collective-permute-start(bf16[16,4,1,1024]{3,2,1,0:T(2,128)(2,1)S(1)} %get-tuple-element.11), channel_id=1, source_target_pairs={{0,4},{4,8},{8,12},{12,16},{16,20},{20,24},{24,28},{1,5},{5,9},{9,... | collective-permute-start | bytes 393224 | tf_op jit(solution)/shard_map/ppermute | solution.py:12
  11.4 5.5 %collective-permute-start.1 = (bf16[16,4,1,1024]{3,2,1,0:T(2,128)(2,1)S(1)}, bf16[16,4,1,1024]{3,2,1,0:T(2,128)(2,1)S(1)}, u32[]{:S(2)}, u32[]{:S(2)}) collective-permute-start(bf16[16,4,1,1024]{3,2,1,0:T(2,128)(2,1)S(1)} %get-tuple-element.12), channel_id=1, source_target_pairs={{4,0},{8,4},{12,8},{16,12},{20,16},{24,20},{28,24},{5,1},{9,5},{13... | collective-permute-start | bytes 393224 | tf_op jit(solution)/shard_map/ppermute | solution.py:15
  17.3 8.9 %collective-permute-start.2 = (bf16[16,1,4,1024]{3,2,1,0:T(4,128)(2,1)S(1)}, bf16[16,1,4,1024]{3,2,1,0:T(4,128)(2,1)S(1)}, u32[]{:S(2)}, u32[]{:S(2)}) collective-permute-start(bf16[16,1,4,1024]{3,2,1,0:T(4,128)(2,1)S(1)} %get-tuple-element.7), channel_id=1, source_target_pairs={{0,1},{1,2},{2,3},{4,5},{5,6},{6,7},{8,9},{9,10},{10,11},{12,13},{... | collective-permute-start | bytes 393224 | tf_op jit(solution)/shard_map/ppermute | solution.py:12
  20.8 10.7 %collective-permute-start.3 = (bf16[16,1,4,1024]{3,2,1,0:T(4,128)(2,1)S(1)}, bf16[16,1,4,1024]{3,2,1,0:T(4,128)(2,1)S(1)}, u32[]{:S(2)}, u32[]{:S(2)}) collective-permute-start(bf16[16,1,4,1024]{3,2,1,0:T(4,128)(2,1)S(1)} %get-tuple-element.8), channel_id=1, source_target_pairs={{1,0},{2,1},{3,2},{5,4},{6,5},{7,6},{9,8},{10,9},{11,10},{13,12},{... | collective-permute-start | bytes 393224 | tf_op jit(solution)/shard_map/ppermute | solution.py:15
  32.5 14.9 %copy-start.3 = (f32[27,1024]{1,0:T(8,128)S(1)}, f32[27,1024]{1,0:T(8,128)}, u32[]{:S(2)}) copy-start(f32[27,1024]{1,0:T(8,128)} %param.7) | copy-start | bytes 331780
  39.9 7.6 %collective-permute-start.4 = (bf16[16,4,1,1024]{3,2,1,0:T(2,128)(2,1)S(1)}, bf16[16,4,1,1024]{3,2,1,0:T(2,128)(2,1)S(1)}, u32[]{:S(2)}, u32[]{:S(2)}) collective-permute-start(bf16[16,4,1,1024]{3,2,1,0:T(2,128)(2,1)S(1)} %get-tuple-element.9), channel_id=1, source_target_pairs={{0,4},{4,8},{8,12},{12,16},{16,20},{20,24},{24,28},{1,5},{5,9},{9,... | collective-permute-start | bytes 393224 | tf_op jit(solution)/shard_map/ppermute | solution.py:12
  46.1 4.1 %collective-permute-start.5 = (bf16[16,4,1,1024]{3,2,1,0:T(2,128)(2,1)S(1)}, bf16[16,4,1,1024]{3,2,1,0:T(2,128)(2,1)S(1)}, u32[]{:S(2)}, u32[]{:S(2)}) collective-permute-start(bf16[16,4,1,1024]{3,2,1,0:T(2,128)(2,1)S(1)} %get-tuple-element.10), channel_id=1, source_target_pairs={{4,0},{8,4},{12,8},{16,12},{20,16},{24,20},{28,24},{5,1},{9,5},{13... | collective-permute-start | bytes 393224 | tf_op jit(solution)/shard_map/ppermute | solution.py:15
  50.7 13.8 %collective-permute-start.6 = (bf16[16,1,4,1024]{3,2,1,0:T(4,128)(2,1)S(1)}, bf16[16,1,4,1024]{3,2,1,0:T(4,128)(2,1)S(1)}, u32[]{:S(2)}, u32[]{:S(2)}) collective-permute-start(bf16[16,1,4,1024]{3,2,1,0:T(4,128)(2,1)S(1)} %get-tuple-element.5), channel_id=1, source_target_pairs={{0,1},{1,2},{2,3},{4,5},{5,6},{6,7},{8,9},{9,10},{10,11},{12,13},{... | collective-permute-start | bytes 393224 | tf_op jit(solution)/shard_map/ppermute | solution.py:12
  59.1 17.6 %collective-permute-start.7 = (bf16[16,1,4,1024]{3,2,1,0:T(4,128)(2,1)S(1)}, bf16[16,1,4,1024]{3,2,1,0:T(4,128)(2,1)S(1)}, u32[]{:S(2)}, u32[]{:S(2)}) collective-permute-start(bf16[16,1,4,1024]{3,2,1,0:T(4,128)(2,1)S(1)} %get-tuple-element.6), channel_id=1, source_target_pairs={{1,0},{2,1},{3,2},{5,4},{6,5},{7,6},{9,8},{10,9},{11,10},{13,12},{... | collective-permute-start | bytes 393224 | tf_op jit(solution)/shard_map/ppermute | solution.py:15
Sparse Core Ops, SparseCore 0:
  8.9 88.8 all-gather.1
  142.6 134.7 all-reduce.3
where the time goes:
time: 289 us; the launch traced here: 288 us
  waiting for transfers between devices  141 us (49%)
  blocking collectives  79.9 us (28%)
  starting transfers between devices  25.8 us (9%)
  other arithmetic  18.7 us (6%)
  between operations  13.6 us (5%)
  matrix products  6.15 us (2%)
  local copies, waits for them, and re-layouts  3.37 us (1%)
    psum x1, waiting for transfers between devices, local(): lax.psum((numerator, denominator), ('slab', 'lat'))  94.3 us
    psum x1, blocking collectives, local(): lax.psum((numerator, denominator), ('slab', 'lat'))  40.4 us
    pmax x1, blocking collectives, local(): maximum = lax.pmax(local_max, ('slab', 'lat'))  39.5 us
    ppermute x4, waiting for transfers between devices, with_halo(): lax.ppermute(lax.slice_in_dim(block, 0, width, axis=dim), axis, backward)  24.4 us
    ppermute x4, starting transfers between devices, with_halo(): lax.ppermute(lax.slice_in_dim(block, block.shape[dim] - width, None, axis...  20.5 us
    all_gather x1, waiting for transfers between devices, local(): lax.all_gather(kv_weight, 'lat', axis=2, tiled=True)  13 us
    ppermute x4, waiting for transfers between devices, with_halo(): lax.ppermute(lax.slice_in_dim(block, block.shape[dim] - width, None, axis...  8.15 us
    convert_element_type x1, other arithmetic, local(): hidden = (source + mixed).astype(jnp.bfloat16)  6.96 us
  transfers between devices with their start and end apart: 10, of which 8 were waited for; matrix products, arithmetic and copies ran while one was open for 7% of the time, Pallas kernels for 0%

commit v1 on v0

--- a/solution.py
+++ b/solution.py
@@ -67,7 +67,7 @@
     weights_bf = exponent.astype(jnp.bfloat16)
     denominator = jnp.sum(exponent, axis=1)
     numerator = jnp.dot(weights_bf, value_rows, preferred_element_type=jnp.float32)
-    numer_total, denom_total = lax.psum((numerator, denominator), ("slab", "lat"))
+    numer_total, denom_total = lax.psum(lax.psum((numerator, denominator), "lat"), "slab")
     latents = (numer_total / denom_total[:, None]).astype(jnp.bfloat16)
     back = (
         jnp.einsum("td,ld->tl", token_rows, latents, preferred_element_type=jnp.float32)

time: 289 us -> 304 us (1.052)
  waiting for transfers between devices: 141 us -> 174 us
  blocking collectives: 79.9 us -> 61.6 us
    psum x1 -> x2, waiting for transfers between devices: 94.3 us -> 128 us  [the longest x1 86 us: local(): lax.psum((numerator, denominator), 'lat')]
    psum x1 -> x2, blocking collectives: 40.4 us -> 22.1 us  [the longest x1 12.1 us: local(): lax.psum(lax.psum((numerator, denominator), 'lat'), 'slab')]
  transfers between devices with their start and end apart: 10 -> 11, of which waited for: 8 -> 9; matrix products, arithmetic and copies ran while one was open for 7% -> 6% of each run, Pallas kernels for 0% -> 0%
where the time goes in v1:
time: 304 us; the launch traced here: 303 us
  waiting for transfers between devices  174 us (57%)
  blocking collectives  61.6 us (20%)
  starting transfers between devices  25.8 us (8%)
  other arithmetic  18.7 us (6%)
  between operations  13.4 us (4%)
  matrix products  6.15 us (2%)
  local copies, waits for them, and re-layouts  3.37 us (1%)
    psum x1, waiting for transfers between devices, local(): lax.psum((numerator, denominator), 'lat')  86 us
    psum x1, waiting for transfers between devices, local(): lax.psum(lax.psum((numerator, denominator), 'lat'), 'slab')  41.9 us
    pmax x1, blocking collectives, local(): maximum = lax.pmax(local_max, ('slab', 'lat'))  39.5 us
    ppermute x4, waiting for transfers between devices, with_halo(): lax.ppermute(lax.slice_in_dim(block, 0, width, axis=dim), axis, backward)  24.4 us
    ppermute x4, starting transfers between devices, with_halo(): lax.ppermute(lax.slice_in_dim(block, block.shape[dim] - width, None, axis...  20.5 us
    all_gather x1, waiting for transfers between devices, local(): lax.all_gather(kv_weight, 'lat', axis=2, tiled=True)  13 us
    psum x1, blocking collectives, local(): lax.psum(lax.psum((numerator, denominator), 'lat'), 'slab')  12.1 us
    psum x1, blocking collectives, local(): lax.psum((numerator, denominator), 'lat')  9.98 us
  transfers between devices with their start and end apart: 11, of which 9 were waited for; matrix products, arithmetic and copies ran while one was open for 6% of the time, Pallas kernels for 0%

profile of v1, /device:TPU:0, one launch (start us, length us, event | category | flops | bytes accessed | tf_op | source)
XLA Modules:
  0.0 303.1 jit_solution(11232818566193787878)
XLA Ops:
  7.3 1.6 fusion.90
  8.9 2.4 collective-permute-start
  11.4 1.3 collective-permute-start.1
  12.7 4.1 %collective-permute-done.1 = bf16[16,4,1,1024]{3,2,1,0:T(2,128)(2,1)S(1)} collective-permute-done((bf16[16,4,1,1024]{3,2,1,0:T(2,128)(2,1)S(1)}, bf16[16,4,1,1024]{3,2,1,0:T(2,128)(2,1)S(1)}, u32[]{:S(2)}, u32[]{:S(2)}) %collective-permute-start.1) | collective-permute-done | bytes 131104 | tf_op jit(solution)/shard_map/ppermute | solution.py:15
  17.3 3.5 %collective-permute-start.2 = (bf16[16,1,4,1024]{3,2,1,0:T(4,128)(2,1)S(1)}, bf16[16,1,4,1024]{3,2,1,0:T(4,128)(2,1)S(1)}, u32[]{:S(2)}, u32[]{:S(2)}) collective-permute-start(bf16[16,1,4,1024]{3,2,1,0:T(4,128)(2,1)S(1)} %get-tuple-element.7), channel_id=1, source_target_pairs={{0,1},{1,2},{2,3},{4,5},{5,6},{6,7},{8,9},{9,10},{10,11},{12,13},{... | collective-permute-start | bytes 393224 | tf_op jit(solution)/shard_map/ppermute | solution.py:12
  22.2 4.1 %collective-permute-done.2 = bf16[16,1,4,1024]{3,2,1,0:T(4,128)(2,1)S(1)} collective-permute-done((bf16[16,1,4,1024]{3,2,1,0:T(4,128)(2,1)S(1)}, bf16[16,1,4,1024]{3,2,1,0:T(4,128)(2,1)S(1)}, u32[]{:S(2)}, u32[]{:S(2)}) %collective-permute-start.2) | collective-permute-done | bytes 131104 | tf_op jit(solution)/shard_map/ppermute | solution.py:12
  26.2 5.3 %collective-permute-done.3 = bf16[16,1,4,1024]{3,2,1,0:T(4,128)(2,1)S(1)} collective-permute-done((bf16[16,1,4,1024]{3,2,1,0:T(4,128)(2,1)S(1)}, bf16[16,1,4,1024]{3,2,1,0:T(4,128)(2,1)S(1)}, u32[]{:S(2)}, u32[]{:S(2)}) %collective-permute-start.3) | collective-permute-done | bytes 131104 | tf_op jit(solution)/shard_map/ppermute | solution.py:15
  32.5 6.8 %fusion.79 = bf16[16,4,2,1024]{3,2,1,0:T(2,128)(2,1)S(1)} fusion(f32[16,6,4,1024]{3,2,1,0:T(4,128)S(1)} %maximum_convert_fusion, f32[1024]{0:T(1024)S(1)} %bitcast.122, f32[1024]{0:T(1024)S(1)} %bitcast.123, f32[1024]{0:T(1024)S(1)} %bitcast.98, f32[1024]{0:T(1024)S(1)} %bitcast.99, f32[1024]{0:T(1024)S(1)} %bitcast.100, f32[1024]{0:T(1024)S(1)} %bitcast.101, ...), kind=kLoop, calls=%fused_computation.126 | loop fusion | flops 8126464 | bytes 6664192 | tf_op jit(solution)/shard_map/convert_element_type | solution.py:44
  39.9 6.2 %collective-permute-start.4 = (bf16[16,4,1,1024]{3,2,1,0:T(2,128)(2,1)S(1)}, bf16[16,4,1,1024]{3,2,1,0:T(2,128)(2,1)S(1)}, u32[]{:S(2)}, u32[]{:S(2)}) collective-permute-start(bf16[16,4,1,1024]{3,2,1,0:T(2,128)(2,1)S(1)} %get-tuple-element.9), channel_id=1, source_target_pairs={{0,4},{4,8},{8,12},{12,16},{16,20},{20,24},{24,28},{1,5},{5,9},{9,... | collective-permute-start | bytes 393224 | tf_op jit(solution)/shard_map/ppermute | solution.py:12
  46.1 1.3 collective-permute-start.5
  47.5 2.7 collective-permute-done.5
  50.7 8.4 %collective-permute-start.6 = (bf16[16,1,4,1024]{3,2,1,0:T(4,128)(2,1)S(1)}, bf16[16,1,4,1024]{3,2,1,0:T(4,128)(2,1)S(1)}, u32[]{:S(2)}, u32[]{:S(2)}) collective-permute-start(bf16[16,1,4,1024]{3,2,1,0:T(4,128)(2,1)S(1)} %get-tuple-element.5), channel_id=1, source_target_pairs={{0,1},{1,2},{2,3},{4,5},{5,6},{6,7},{8,9},{9,10},{10,11},{12,13},{... | collective-permute-start | bytes 393224 | tf_op jit(solution)/shard_map/ppermute | solution.py:12
  60.4 4.1 %collective-permute-done.6 = bf16[16,1,4,1024]{3,2,1,0:T(4,128)(2,1)S(1)} collective-permute-done((bf16[16,1,4,1024]{3,2,1,0:T(4,128)(2,1)S(1)}, bf16[16,1,4,1024]{3,2,1,0:T(4,128)(2,1)S(1)}, u32[]{:S(2)}, u32[]{:S(2)}) %collective-permute-start.6) | collective-permute-done | bytes 131104 | tf_op jit(solution)/shard_map/ppermute | solution.py:12
  64.5 12.2 %collective-permute-done.7 = bf16[16,1,4,1024]{3,2,1,0:T(4,128)(2,1)S(1)} collective-permute-done((bf16[16,1,4,1024]{3,2,1,0:T(4,128)(2,1)S(1)}, bf16[16,1,4,1024]{3,2,1,0:T(4,128)(2,1)S(1)}, u32[]{:S(2)}, u32[]{:S(2)}) %collective-permute-start.7) | collective-permute-done | bytes 131104 | tf_op jit(solution)/shard_map/ppermute | solution.py:15
  77.7 7.0 %fusion.80 = bf16[16,4,2,1024]{3,2,1,0:T(2,128)(2,1)S(1)} fusion(f32[16,6,4,1024]{3,2,1,0:T(4,128)S(1)} %maximum_convert_fusion.1, bf16[16,4,2,1024]{3,2,1,0:T(2,128)(2,1)S(1)} %copy-done.1, f32[1024]{0:T(1024)S(1)} %bitcast.95, f32[1024]{0:T(1024)S(1)} %bitcast.96, f32[1024]{0:T(1024)S(1)} %bitcast.71, f32[1024]{0:T(1024)S(1)} %bitcast.72, ...), kind=kLoop, calls=%fused_computation.127 | loop fusion | flops 8388608 | bytes 6926336 | tf_op jit(solution)/shard_map/convert_element_type | solution.py:49
  84.8 13.0 %all-gather.2.cloned.1.call-done = bf16[2,1024,1024]{2,1,0:T(8,128)(2,1)} async-done(((bf16[2,1024,256]{2,1,0:T(8,128)(2,1)}), bf16[2,1024,1024]{2,1,0:T(8,128)(2,1)}) %all-gather.2.cloned.1.call-update) | async-done | bytes 4194320 | tf_op jit(solution)/shard_map/all_gather | solution.py:54
  97.8 2.9 fusion
  101.2 39.5 %pmax.7 = f32[512]{0:T(512)S(1)} all-reduce(f32[512]{0:T(512)S(1)} %get-tuple-element.67), channel_id=1, replica_groups=mesh['slab'=8,'lat'=4] {'slab','lat'}, use_global_device_ids=true, to_apply=%region_1.2 | all-reduce | flops 512 | bytes 4096 | tf_op jit(solution)/shard_map/pmax | solution.py:65
  140.7 1.8 fusion.81
  142.5 86.0 %all-reduce.5.cloned.1.call-done = f32[512,1024]{1,0:T(8,128)} async-done(((f32[512,1024]{1,0:T(8,128)}), f32[512,1024]{1,0:T(8,128)}) %all-reduce.5.cloned.1.call-update) | async-done | bytes 2097168 | tf_op jit(solution)/shard_map/psum | solution.py:70
  228.7 10.0 %psum.30 = f32[512]{0:T(512)S(1)} all-reduce(f32[512]{0:T(512)S(1)} %fusion.82), channel_id=1, replica_groups=mesh['slab'=8,'lat'=4] {'lat'}, use_global_device_ids=true, to_apply=%region_5.6 | all-reduce | flops 512 | bytes 4096 | tf_op jit(solution)/shard_map/psum | solution.py:70
  238.7 12.1 %psum.31 = f32[512]{0:T(512)S(1)} all-reduce(f32[512]{0:T(512)S(1)} %psum.30), channel_id=1, replica_groups=mesh['slab'=8,'lat'=4] {'slab'}, use_global_device_ids=true, to_apply=%region_6.7 | all-reduce | flops 512 | bytes 4096 | tf_op jit(solution)/shard_map/psum | solution.py:70
  250.8 41.9 %all-reduce.7.cloned.1.call-done = f32[512,1024]{1,0:T(8,128)} async-done(((f32[512,1024]{1,0:T(8,128)}), f32[512,1024]{1,0:T(8,128)}) %all-reduce.7.cloned.1.call-update) | async-done | bytes 2097168 | tf_op jit(solution)/shard_map/psum | solution.py:70
  292.7 1.9 divide_convert_fusion
  (35 shorter events, 9.7 us)
Async XLA Ops:
  6.5 94.1 %copy-start = (bf16[512,1024]{1,0:T(8,128)(2,1)S(1)}, bf16[512,1024]{1,0:T(8,128)(2,1)}, u32[]{:S(2)}) copy-start(bf16[512,1024]{1,0:T(8,128)(2,1)} %param.9) | copy-start | bytes 3145732
  6.5 10.3 %copy-start.1 = (bf16[16,4,2,1024]{3,2,1,0:T(2,128)(2,1)S(1)}, bf16[16,4,2,1024]{3,2,1,0:T(2,128)(2,1)}, u32[]{:S(2)}) copy-start(bf16[16,4,2,1024]{3,2,1,0:T(2,128)(2,1)} %param.5) | copy-start | bytes 786436
  6.5 6.1 %copy-start.2 = (f32[27,1024]{1,0:T(8,128)S(1)}, f32[27,1024]{1,0:T(8,128)}, u32[]{:S(2)}) copy-start(f32[27,1024]{1,0:T(8,128)} %param.6) | copy-start | bytes 331780
  6.5 91.2 %all-gather.2.cloned.1.call-start = ((), (), s32[]{:S(2)}) async-start(), calls=%async_computation | async-start | bytes 5242880 | tf_op jit(solution)/shard_map/all_gather | solution.py:54
  7.3 221.3 %all-reduce.5.cloned.1.call-start = ((), (), s32[]{:S(2)}) async-start(), calls=%async_computation.1 | async-start | bytes 4194304 | tf_op jit(solution)/shard_map/psum | solution.py:70
  8.9 3.8 %collective-permute-start = (bf16[16,4,1,1024]{3,2,1,0:T(2,128)(2,1)S(1)}, bf16[16,4,1,1024]{3,2,1,0:T(2,128)(2,1)S(1)}, u32[]{:S(2)}, u32[]{:S(2)}) collective-permute-start(bf16[16,4,1,1024]{3,2,1,0:T(2,128)(2,1)S(1)} %get-tuple-element.11), channel_id=1, source_target_pairs={{0,4},{4,8},{8,12},{12,16},{16,20},{20,24},{24,28},{1,5},{5,9},{9,... | collective-permute-start | bytes 393224 | tf_op jit(solution)/shard_map/ppermute | solution.py:12
  11.4 5.5 %collective-permute-start.1 = (bf16[16,4,1,1024]{3,2,1,0:T(2,128)(2,1)S(1)}, bf16[16,4,1,1024]{3,2,1,0:T(2,128)(2,1)S(1)}, u32[]{:S(2)}, u32[]{:S(2)}) collective-permute-start(bf16[16,4,1,1024]{3,2,1,0:T(2,128)(2,1)S(1)} %get-tuple-element.12), channel_id=1, source_target_pairs={{4,0},{8,4},{12,8},{16,12},{20,16},{24,20},{28,24},{5,1},{9,5},{13... | collective-permute-start | bytes 393224 | tf_op jit(solution)/shard_map/ppermute | solution.py:15
  17.3 8.9 %collective-permute-start.2 = (bf16[16,1,4,1024]{3,2,1,0:T(4,128)(2,1)S(1)}, bf16[16,1,4,1024]{3,2,1,0:T(4,128)(2,1)S(1)}, u32[]{:S(2)}, u32[]{:S(2)}) collective-permute-start(bf16[16,1,4,1024]{3,2,1,0:T(4,128)(2,1)S(1)} %get-tuple-element.7), channel_id=1, source_target_pairs={{0,1},{1,2},{2,3},{4,5},{5,6},{6,7},{8,9},{9,10},{10,11},{12,13},{... | collective-permute-start | bytes 393224 | tf_op jit(solution)/shard_map/ppermute | solution.py:12
  20.8 10.7 %collective-permute-start.3 = (bf16[16,1,4,1024]{3,2,1,0:T(4,128)(2,1)S(1)}, bf16[16,1,4,1024]{3,2,1,0:T(4,128)(2,1)S(1)}, u32[]{:S(2)}, u32[]{:S(2)}) collective-permute-start(bf16[16,1,4,1024]{3,2,1,0:T(4,128)(2,1)S(1)} %get-tuple-element.8), channel_id=1, source_target_pairs={{1,0},{2,1},{3,2},{5,4},{6,5},{7,6},{9,8},{10,9},{11,10},{13,12},{... | collective-permute-start | bytes 393224 | tf_op jit(solution)/shard_map/ppermute | solution.py:15
  32.5 14.9 %copy-start.3 = (f32[27,1024]{1,0:T(8,128)S(1)}, f32[27,1024]{1,0:T(8,128)}, u32[]{:S(2)}) copy-start(f32[27,1024]{1,0:T(8,128)} %param.7) | copy-start | bytes 331780
  39.9 7.6 %collective-permute-start.4 = (bf16[16,4,1,1024]{3,2,1,0:T(2,128)(2,1)S(1)}, bf16[16,4,1,1024]{3,2,1,0:T(2,128)(2,1)S(1)}, u32[]{:S(2)}, u32[]{:S(2)}) collective-permute-start(bf16[16,4,1,1024]{3,2,1,0:T(2,128)(2,1)S(1)} %get-tuple-element.9), channel_id=1, source_target_pairs={{0,4},{4,8},{8,12},{12,16},{16,20},{20,24},{24,28},{1,5},{5,9},{9,... | collective-permute-start | bytes 393224 | tf_op jit(solution)/shard_map/ppermute | solution.py:12
  46.1 4.1 %collective-permute-start.5 = (bf16[16,4,1,1024]{3,2,1,0:T(2,128)(2,1)S(1)}, bf16[16,4,1,1024]{3,2,1,0:T(2,128)(2,1)S(1)}, u32[]{:S(2)}, u32[]{:S(2)}) collective-permute-start(bf16[16,4,1,1024]{3,2,1,0:T(2,128)(2,1)S(1)} %get-tuple-element.10), channel_id=1, source_target_pairs={{4,0},{8,4},{12,8},{16,12},{20,16},{24,20},{28,24},{5,1},{9,5},{13... | collective-permute-start | bytes 393224 | tf_op jit(solution)/shard_map/ppermute | solution.py:15
  50.7 13.8 %collective-permute-start.6 = (bf16[16,1,4,1024]{3,2,1,0:T(4,128)(2,1)S(1)}, bf16[16,1,4,1024]{3,2,1,0:T(4,128)(2,1)S(1)}, u32[]{:S(2)}, u32[]{:S(2)}) collective-permute-start(bf16[16,1,4,1024]{3,2,1,0:T(4,128)(2,1)S(1)} %get-tuple-element.5), channel_id=1, source_target_pairs={{0,1},{1,2},{2,3},{4,5},{5,6},{6,7},{8,9},{9,10},{10,11},{12,13},{... | collective-permute-start | bytes 393224 | tf_op jit(solution)/shard_map/ppermute | solution.py:12
  59.1 17.6 %collective-permute-start.7 = (bf16[16,1,4,1024]{3,2,1,0:T(4,128)(2,1)S(1)}, bf16[16,1,4,1024]{3,2,1,0:T(4,128)(2,1)S(1)}, u32[]{:S(2)}, u32[]{:S(2)}) collective-permute-start(bf16[16,1,4,1024]{3,2,1,0:T(4,128)(2,1)S(1)} %get-tuple-element.6), channel_id=1, source_target_pairs={{1,0},{2,1},{3,2},{5,4},{6,5},{7,6},{9,8},{10,9},{11,10},{13,12},{... | collective-permute-start | bytes 393224 | tf_op jit(solution)/shard_map/ppermute | solution.py:15
  142.5 150.2 %all-reduce.7.cloned.1.call-start = ((), (), s32[]{:S(2)}) async-start(), calls=%async_computation.2 | async-start | bytes 4194304 | tf_op jit(solution)/shard_map/psum | solution.py:70
Sparse Core Ops, SparseCore 0:
  8.9 88.8 all-gather.1
  142.6 85.8 all-reduce.4
  231.8 60.8 all-reduce.6
